TPU v7x, 32 devices: a whole 2x2x4 slice. The times are simulated.
32 devices in a mesh: grp: 2 (over x), res: 16 (over z, y, core).
Axes of the slice: x: 2, y: 2, z: 4, core: 2. Of those that a mesh axis runs over, the one named last changes fastest.
Arguments:
- stacked_sequence_embedding: bfloat16 [1024, 8192], P(('grp', 'res')), parts along dimension 0, may hold values from -6 to 6
- normalizer_multiplier: float32 [64], replicated, may hold values from 0.1 to 1.9
- normalizer_additive: float32 [64], replicated, may hold values from -2 to 2
- lhs_projected_tensor: bfloat16 [64, 32], replicated, may hold values from -0.75 to 0.75
- rhs_projected_tensor: bfloat16 [64, 32], replicated, may hold values from -0.75 to 0.75
- pairwise_matrix: bfloat16 [1024, 128], replicated, may hold values from -0.359375 to 0.359375
- pairwise_shift: float32 [128], replicated, may hold values from -3 to 3
Outputs:
- pair_update: bfloat16 [256, 128, 128], P(('grp', 'res')), parts along dimension 0
There are 2 independent parts, one for each index of `grp`. A program takes and returns all parts, laid end to end along the dimension named above; an argument that names none is the same for every part. Nothing has to cross between parts.
All inputs are finite; a program needn't handle non-finite values.
Results may differ from a plain program's by a relative error of at most 0.0047.
Values may be sent and summed in bfloat16 or wider, within the bound.
A program may use at most 128 MiB of HBM per device.

v0:
```python
import jax
import jax.numpy as jnp
from jax import lax
from jax.sharding import PartitionSpec as P


def normalize(member_list, normalizer_multiplier, normalizer_additive):
    center = member_list - jnp.mean(member_list, axis=-1, keepdims=True)
    spread = jnp.mean(center * center, axis=-1, keepdims=True)
    return (
        center * lax.rsqrt(spread + 1e-05) * normalizer_multiplier + normalizer_additive
    ).astype(jnp.bfloat16)


def project_both(
    member_list,
    normalizer_multiplier,
    normalizer_additive,
    lhs_projected_tensor,
    rhs_projected_tensor,
    rows,
    residues,
):
    chans = lhs_projected_tensor.shape[0]
    width = lhs_projected_tensor.shape[1]
    normed = normalize(
        member_list.astype(jnp.float32).reshape(rows * residues, chans),
        normalizer_multiplier,
        normalizer_additive,
    )
    left = (
        jnp.dot(normed, lhs_projected_tensor, preferred_element_type=jnp.float32)
        .astype(jnp.bfloat16)
        .reshape(rows, residues * width)
    )
    right = (
        jnp.dot(normed, rhs_projected_tensor, preferred_element_type=jnp.float32)
        .astype(jnp.bfloat16)
        .reshape(rows, residues * width)
    )
    return (left, right)


def pair_block(left, piece, pairwise_matrix, pairwise_shift, width):
    rows = left.shape[0]
    left_count = left.shape[1] // width
    right_count = piece.shape[1] // width
    outer = (
        lax.dot_general(left, piece, (((0,), (0,)), ((), ())), preferred_element_type=jnp.float32)
        / rows
    )
    flat = outer.reshape(left_count, width, right_count, width).transpose(0, 2, 1, 3)
    flat = flat.reshape(left_count * right_count, width * width).astype(jnp.bfloat16)
    mapped = jnp.dot(flat, pairwise_matrix, preferred_element_type=jnp.float32) + pairwise_shift
    return mapped.astype(jnp.bfloat16).reshape(left_count, right_count, pairwise_matrix.shape[1])


def on_device(
    stacked_sequence_embedding,
    normalizer_multiplier,
    normalizer_additive,
    lhs_projected_tensor,
    rhs_projected_tensor,
    pairwise_matrix,
    pairwise_shift,
):
    chans = lhs_projected_tensor.shape[0]
    width = lhs_projected_tensor.shape[1]
    partition_numbers = lax.all_to_all(
        stacked_sequence_embedding, "res", split_axis=1, concat_axis=0, tiled=True
    )
    rows = partition_numbers.shape[0]
    resid = partition_numbers.shape[1] // chans
    left, right = project_both(
        partition_numbers,
        normalizer_multiplier,
        normalizer_additive,
        lhs_projected_tensor,
        rhs_projected_tensor,
        rows,
        resid,
    )
    return pair_block(
        left,
        lax.all_gather(right, "res", axis=1, tiled=True),
        pairwise_matrix,
        pairwise_shift,
        width,
    )


def solution(mesh):
    in_specs = (P(("grp", "res"), None), P(), P(), P(), P(), P(), P())
    out_specs = P(("grp", "res"), None, None)
    return jax.shard_map(
        on_device, mesh=mesh, in_specs=in_specs, out_specs=out_specs, check_vma=False
    )
```

profile of v0, /device:TPU:0, one launch (start us, length us, event | category | flops | bytes accessed | tf_op | source)
XLA Modules:
  0.0 116.2 jit_solution(17071124105977982926)
XLA Ops:
  6.5 0.0 copy-start
  6.5 0.0 all-gather.2.cloned.1.call-start
  6.5 1.1 copy.23
  7.7 21.7 %all_to_all.13 = bf16[32,16,512]{2,0,1:T(8,128)(2,1)S(1)} all-to-all(bf16[32,16,512]{2,0,1:T(8,128)(2,1)S(1)} %bitcast.28), channel_id=1, replica_groups=mesh['grp'=2,'res'=16] {'res'}, dimensions={1} | all-to-all | bytes 1048576 | tf_op jit(solution)/shard_map/all_to_all | solution.py:69
  29.3 0.1 convert_bitcast_fusion
  29.5 0.4 reshape.38
  29.9 0.0 copy-start.3
  29.9 0.0 copy-start.4
  29.9 0.6 reduce_sum.18
  30.5 1.3 %multiply_reduce_fusion = f32[4096]{0:T(1024)S(1)} fusion(f32[4096,64]{1,0:T(8,128)S(1)} %reshape.38, f32[4096]{0:T(1024)S(1)} %broadcast_multiply_fusion), kind=kLoop, calls=%fused_computation.8 | loop fusion | flops 782336 | bytes 1081344 | tf_op jit(solution)/shard_map/reduce_sum | solution.py:9
  31.8 0.0 copy-start.1
  31.8 0.0 copy-done.3
  31.9 0.0 copy-done.4
  31.9 2.3 %add_convert_fusion = bf16[4096,64]{1,0:T(8,128)(2,1)S(1)} fusion(f32[4096,64]{1,0:T(8,128)S(1)} %reshape.38, f32[64]{0:T(128)S(1)} %copy-done.3, f32[64]{0:T(128)S(1)} %copy-done.4, f32[4096]{0:T(1024)S(1)} %add_rsqrt_fusion, f32[4096]{0:T(1024)S(1)} %broadcast_multiply_fusion), kind=kLoop, calls=%fused_computation.7 | loop fusion | flops 1310720 | bytes 1606144 | tf_op jit(solution)/shard_map/convert_element_type | solution.py:12
  34.2 0.0 copy-done.1
  34.2 0.0 copy-start.2
  34.2 0.4 convolution_convert_fusion
  34.6 0.5 copy.10
  35.1 1.4 %reshape.36 = bf16[512,256]{1,0:T(8,128)(2,1)} reshape(bf16[4096,32]{1,0:T(8,128)(2,1)S(1)} %copy.10) | data formatting | bytes 524288 | tf_op jit(solution)/shard_map/reshape | solution.py:39
  36.6 0.0 all-gather.2.cloned.1.call-update
  36.6 0.0 copy-done.2
  36.6 0.4 convolution_convert_fusion.1
  37.1 0.5 copy.9
  37.6 0.7 reshape.35
  38.3 51.1 %all-gather.2.cloned.1.call-done = bf16[512,4096]{1,0:T(8,128)(2,1)} async-done(((bf16[512,256]{1,0:T(8,128)(2,1)}), bf16[512,4096]{1,0:T(8,128)(2,1)}) %all-gather.2.cloned.1.call-update) | async-done | bytes 4194320 | tf_op jit(solution)/shard_map/all_gather | solution.py:85
  89.4 3.5 %fusion = bf16[256,4096]{1,0:T(8,128)(2,1)S(1)} fusion(bf16[512,256]{1,0:T(8,128)(2,1)S(1)} %reshape.35, bf16[512,4096]{1,0:T(8,128)(2,1)} %all-gather.2.cloned.1.call-done), kind=kOutput, calls=%fused_computation.1 | convolution fusion | flops 1075838976 | bytes 6553600 | tf_op jit(solution)/shard_map/dot_general | solution.py:49
  92.9 8.0 %convert_element_type.41 = bf16[8,32,128,32]{3,2,1,0:T(8,128)(2,1)} reshape(bf16[256,4096]{1,0:T(8,128)(2,1)S(1)} %fusion) | data formatting | bytes 4194304 | tf_op jit(solution)/shard_map/convert_element_type | solution.py:53
  100.9 0.0 copy-start.5
  100.9 7.0 %copy.11 = bf16[8,128,32,32]{1,0,3,2:T(8,128)(2,1)S(1)} copy(bf16[8,128,32,32]{3,1,2,0:T(8,128)(2,1)} %bitcast.26) | data formatting | bytes 4194304 | tf_op jit(solution)/shard_map/convert_element_type | solution.py:53
  107.9 0.0 copy-done
  107.9 0.0 copy-done.5
  107.9 1.5 %fusion.7 = bf16[1024,128]{1,0:T(8,128)(2,1)} fusion(bf16[1024,128]{1,0:T(8,128)(2,1)S(1)} %copy-done, bf16[128,8,8,128]{3,2,1,0:T(8,128)(2,1)S(1)} %bitcast.27, f32[128]{0:T(128)S(1)} %copy-done.5), kind=kOutput, calls=%fused_computation.10 | convolution fusion | flops 268697600 | bytes 2621952 | tf_op jit(solution)/shard_map/dot_general | solution.py:54
  (2 shorter events, 0.0 us)
Async XLA Ops:
  6.5 101.3 %copy-start = (bf16[1024,128]{1,0:T(8,128)(2,1)S(1)}, bf16[1024,128]{1,0:T(8,128)(2,1)}, u32[]{:S(2)}) copy-start(bf16[1024,128]{1,0:T(8,128)(2,1)} %param.12) | copy-start | bytes 786436
  6.5 82.8 %all-gather.2.cloned.1.call-start = ((), (), s32[]{:S(2)}) async-start(), calls=%async_computation.1 | async-start | bytes 4456448 | tf_op jit(solution)/shard_map/all_gather | solution.py:85
  29.9 2.0 %copy-start.3 = (f32[64]{0:T(128)S(1)}, f32[64]{0:T(128)}, u32[]{:S(2)}) copy-start(f32[64]{0:T(128)} %param.9) | copy-start | bytes 772
  29.9 2.0 %copy-start.4 = (f32[64]{0:T(128)S(1)}, f32[64]{0:T(128)}, u32[]{:S(2)}) copy-start(f32[64]{0:T(128)} %param.8) | copy-start | bytes 772
  31.8 2.4 %copy-start.1 = (bf16[64,32]{0,1:T(8,128)(2,1)S(1)}, bf16[64,32]{0,1:T(8,128)(2,1)}, u32[]{:S(2)}) copy-start(bf16[64,32]{0,1:T(8,128)(2,1)} %param.11) | copy-start | bytes 12292
  34.2 2.4 %copy-start.2 = (bf16[64,32]{0,1:T(8,128)(2,1)S(1)}, bf16[64,32]{0,1:T(8,128)(2,1)}, u32[]{:S(2)}) copy-start(bf16[64,32]{0,1:T(8,128)(2,1)} %param.10) | copy-start | bytes 12292
  100.9 7.0 %copy-start.5 = (f32[128]{0:T(128)S(1)}, f32[128]{0:T(128)}, u32[]{:S(2)}) copy-start(f32[128]{0:T(128)} %param.13) | copy-start | bytes 1540
Sparse Core Ops, SparseCore 0:
  36.7 52.6 all-gather.1
where the time goes:
time: 117 us; the launch traced here: 116 us
  waiting for transfers between devices  51.1 us (44%)
  blocking collectives  21.7 us (19%)
  local copies, waits for them, and re-layouts  19.7 us (17%)
  between operations  13.6 us (12%)
  matrix products  5.84 us (5%)
  other arithmetic  4.31 us (4%)
    all_gather x1, waiting for transfers between devices, on_device(): lax.all_gather(right, 'res', axis=1, tiled=True)  51.1 us
    all_to_all x1, blocking collectives, on_device(): lax.all_to_all(stacked_sequence_embedding, 'res', split_axis=1, concat_ax...  21.7 us
    convert_element_type x2, local copies, waits for them, and re-layouts, pair_block(): flat.reshape(left_count * right_count, width * width).astype(jnp.bfloat16)  15 us
    dot_general x1, matrix products, pair_block(): lax.dot_general(left, piece, (((0,), (0,)), ((), ())), preferred_element_...  3.47 us
  transfers between devices with their start and end apart: 1, of which 1 were waited for; matrix products, arithmetic and copies ran while one was open for 1% of the time, Pallas kernels for 0%

commit v1 on v0

--- a/solution.py
+++ b/solution.py
@@ -66,9 +66,10 @@
 ):
     chans = lhs_projected_tensor.shape[0]
     width = lhs_projected_tensor.shape[1]
-    partition_numbers = lax.all_to_all(
-        stacked_sequence_embedding, "res", split_axis=1, concat_axis=0, tiled=True
-    )
+    devices = lax.axis_size("res")
+    pieces = jnp.stack(jnp.split(stacked_sequence_embedding, devices, axis=1), axis=0)
+    pieces = lax.all_to_all(pieces, "res", split_axis=0, concat_axis=0)
+    partition_numbers = jnp.concatenate(pieces, axis=0)
     rows = partition_numbers.shape[0]
     resid = partition_numbers.shape[1] // chans
     left, right = project_both(

time: 117 us -> 128 us (1.094)
  local copies, waits for them, and re-layouts: 19.7 us -> 30.8 us
    unnamed x12 -> x27, local copies, waits for them, and re-layouts: 0.03 us -> 11.5 us
where the time goes in v1:
time: 128 us; the launch traced here: 127 us
  waiting for transfers between devices  51.1 us (40%)
  local copies, waits for them, and re-layouts  30.8 us (24%)
  blocking collectives  21.6 us (17%)
  between operations  13.6 us (11%)
  matrix products  5.84 us (5%)
  other arithmetic  4.2 us (3%)
    all_gather x1, waiting for transfers between devices, on_device(): lax.all_gather(right, 'res', axis=1, tiled=True)  51.1 us
    all_to_all x1, blocking collectives, on_device(): pieces = lax.all_to_all(pieces, 'res', split_axis=0, concat_axis=0)  21.6 us
    convert_element_type x2, local copies, waits for them, and re-layouts, pair_block(): flat.reshape(left_count * right_count, width * width).astype(jnp.bfloat16)  15 us
    unnamed x27, local copies, waits for them, and re-layouts  11.5 us
    dot_general x1, matrix products, pair_block(): lax.dot_general(left, piece, (((0,), (0,)), ((), ())), preferred_element_...  3.47 us
  transfers between devices with their start and end apart: 1, of which 1 were waited for; matrix products, arithmetic and copies ran while one was open for 1% of the time, Pallas kernels for 0%

profile of v1, /device:TPU:0, one launch (start us, length us, event | category | flops | bytes accessed | tf_op | source)
XLA Modules:
  0.0 127.2 jit_solution(2069086437250552977)
XLA Ops:
  6.5 0.0 copy-start
  6.5 0.0 all-gather.2.cloned.1.call-start
  6.5 0.8 constant_dynamic-update-slice_fusion.15
  7.3 0.8 constant_dynamic-update-slice_fusion.14
  8.1 0.8 constant_dynamic-update-slice_fusion.13
  8.9 0.8 constant_dynamic-update-slice_fusion.12
  9.6 0.8 constant_dynamic-update-slice_fusion.11
  10.4 0.8 constant_dynamic-update-slice_fusion.10
  11.1 0.8 constant_dynamic-update-slice_fusion.9
  11.9 0.8 constant_dynamic-update-slice_fusion.8
  12.7 0.8 constant_dynamic-update-slice_fusion.7
  13.4 0.8 constant_dynamic-update-slice_fusion.6
  14.2 0.8 constant_dynamic-update-slice_fusion.5
  14.9 0.8 constant_dynamic-update-slice_fusion.4
  15.7 0.8 constant_dynamic-update-slice_fusion.3
  16.5 0.8 constant_dynamic-update-slice_fusion.2
  17.2 0.8 constant_dynamic-update-slice_fusion.1
  18.0 0.8 constant_dynamic-update-slice_fusion
  18.8 21.6 %all_to_all.5 = bf16[16,32,512]{2,1,0:T(8,128)(2,1)S(1)} all-to-all(bf16[16,32,512]{2,1,0:T(8,128)(2,1)S(1)} %constant_dynamic-update-slice_fusion), channel_id=1, replica_groups=mesh['grp'=2,'res'=16] {'res'}, dimensions={0} | all-to-all | bytes 1048576 | tf_op jit(solution)/shard_map/all_to_all | solution.py:71
  40.4 0.4 reshape.36
  40.8 0.0 copy-start.3
  40.8 0.0 copy-start.4
  40.8 0.6 reduce_sum.18
  41.5 1.3 %multiply_reduce_fusion = f32[4096]{0:T(1024)S(1)} fusion(f32[4096,64]{1,0:T(8,128)S(1)} %reshape.36, f32[4096]{0:T(1024)S(1)} %broadcast_multiply_fusion), kind=kLoop, calls=%fused_computation.8 | loop fusion | flops 782336 | bytes 1081344 | tf_op jit(solution)/shard_map/reduce_sum | solution.py:9
  42.8 0.0 copy-start.1
  42.8 0.0 copy-done.3
  42.8 0.0 copy-done.4
  42.8 2.3 %add_convert_fusion = bf16[4096,64]{1,0:T(8,128)(2,1)S(1)} fusion(f32[4096,64]{1,0:T(8,128)S(1)} %reshape.36, f32[64]{0:T(128)S(1)} %copy-done.3, f32[64]{0:T(128)S(1)} %copy-done.4, f32[4096]{0:T(1024)S(1)} %add_rsqrt_fusion, f32[4096]{0:T(1024)S(1)} %broadcast_multiply_fusion), kind=kLoop, calls=%fused_computation.7 | loop fusion | flops 1310720 | bytes 1606144 | tf_op jit(solution)/shard_map/convert_element_type | solution.py:12
  45.1 0.0 copy-done.1
  45.1 0.0 copy-start.2
  45.1 0.4 convolution_convert_fusion
  45.6 0.5 copy.9
  46.1 1.4 %reshape.34 = bf16[512,256]{1,0:T(8,128)(2,1)} reshape(bf16[4096,32]{1,0:T(8,128)(2,1)S(1)} %copy.9) | data formatting | bytes 524288 | tf_op jit(solution)/shard_map/reshape | solution.py:39
  47.5 0.0 all-gather.2.cloned.1.call-update
  47.5 0.0 copy-done.2
  47.5 0.4 convolution_convert_fusion.1
  48.0 0.5 copy.8
  48.5 0.7 reshape.33
  49.2 51.1 %all-gather.2.cloned.1.call-done = bf16[512,4096]{1,0:T(8,128)(2,1)} async-done(((bf16[512,256]{1,0:T(8,128)(2,1)}), bf16[512,4096]{1,0:T(8,128)(2,1)}) %all-gather.2.cloned.1.call-update) | async-done | bytes 4194320 | tf_op jit(solution)/shard_map/all_gather | solution.py:86
  100.3 3.5 %fusion = bf16[256,4096]{1,0:T(8,128)(2,1)S(1)} fusion(bf16[512,256]{1,0:T(8,128)(2,1)S(1)} %reshape.33, bf16[512,4096]{1,0:T(8,128)(2,1)} %all-gather.2.cloned.1.call-done), kind=kOutput, calls=%fused_computation.1 | convolution fusion | flops 1075838976 | bytes 6553600 | tf_op jit(solution)/shard_map/dot_general | solution.py:49
  103.8 8.0 %convert_element_type.37 = bf16[8,32,128,32]{3,2,1,0:T(8,128)(2,1)} reshape(bf16[256,4096]{1,0:T(8,128)(2,1)S(1)} %fusion) | data formatting | bytes 4194304 | tf_op jit(solution)/shard_map/convert_element_type | solution.py:53
  111.8 0.0 copy-start.5
  111.8 7.0 %copy.10 = bf16[8,128,32,32]{1,0,3,2:T(8,128)(2,1)S(1)} copy(bf16[8,128,32,32]{3,1,2,0:T(8,128)(2,1)} %bitcast.52) | data formatting | bytes 4194304 | tf_op jit(solution)/shard_map/convert_element_type | solution.py:53
  118.8 0.0 copy-done
  118.8 0.0 copy-done.5
  118.8 1.5 %fusion.7 = bf16[1024,128]{1,0:T(8,128)(2,1)} fusion(bf16[1024,128]{1,0:T(8,128)(2,1)S(1)} %copy-done, bf16[128,8,8,128]{3,2,1,0:T(8,128)(2,1)S(1)} %bitcast.53, f32[128]{0:T(128)S(1)} %copy-done.5), kind=kOutput, calls=%fused_computation.10 | convolution fusion | flops 268697600 | bytes 2621952 | tf_op jit(solution)/shard_map/dot_general | solution.py:54
  (2 shorter events, 0.0 us)
Async XLA Ops:
  6.5 112.3 %copy-start = (bf16[1024,128]{1,0:T(8,128)(2,1)S(1)}, bf16[1024,128]{1,0:T(8,128)(2,1)}, u32[]{:S(2)}) copy-start(bf16[1024,128]{1,0:T(8,128)(2,1)} %param.12) | copy-start | bytes 786436
  6.5 93.8 %all-gather.2.cloned.1.call-start = ((), (), s32[]{:S(2)}) async-start(), calls=%async_computation.1 | async-start | bytes 4456448 | tf_op jit(solution)/shard_map/all_gather | solution.py:86
  40.8 2.0 %copy-start.3 = (f32[64]{0:T(128)S(1)}, f32[64]{0:T(128)}, u32[]{:S(2)}) copy-start(f32[64]{0:T(128)} %param.9) | copy-start | bytes 772
  40.8 2.0 %copy-start.4 = (f32[64]{0:T(128)S(1)}, f32[64]{0:T(128)}, u32[]{:S(2)}) copy-start(f32[64]{0:T(128)} %param.8) | copy-start | bytes 772
  42.8 2.4 %copy-start.1 = (bf16[64,32]{0,1:T(8,128)(2,1)S(1)}, bf16[64,32]{0,1:T(8,128)(2,1)}, u32[]{:S(2)}) copy-start(bf16[64,32]{0,1:T(8,128)(2,1)} %param.11) | copy-start | bytes 12292
  45.1 2.4 %copy-start.2 = (bf16[64,32]{0,1:T(8,128)(2,1)S(1)}, bf16[64,32]{0,1:T(8,128)(2,1)}, u32[]{:S(2)}) copy-start(bf16[64,32]{0,1:T(8,128)(2,1)} %param.10) | copy-start | bytes 12292
  111.8 7.0 %copy-start.5 = (f32[128]{0:T(128)S(1)}, f32[128]{0:T(128)}, u32[]{:S(2)}) copy-start(f32[128]{0:T(128)} %param.13) | copy-start | bytes 1540
Sparse Core Ops, SparseCore 0:
  47.7 52.6 all-gather.1
